TPU v7x, 32 devices: a whole 2x2x4 slice. The times are simulated.
32 devices in a mesh: ctx: 16 (over z, y, x), dp: 2 (over core).
Axes of the slice: x: 2, y: 2, z: 4, core: 2. Of those that a mesh axis runs over, the one named last changes fastest.
Arguments:
- inputs: bfloat16 [2, 2048, 12288], P('dp', 'ctx'), may hold values from -6 to 6
- feat_weight: float32 [7, 12288], P(None, 'dp'), may hold values from -2 to 2
- filter_taps: float32 [128, 4096], P(None, 'dp'), may hold values from -0.5 to 0.5
- upstream: bfloat16 [2, 2048, 4096], P('dp', 'ctx'), may hold values from -6 to 6
Outputs:
- filter_grad: float32 [128, 4096], P(None, 'dp')
- feat_grad: float32 [7, 12288], P(None, 'dp')
All inputs are finite; a program needn't handle non-finite values.
Results may differ from a plain program's by a relative error of at most 0.0041.
Values may be sent and summed in bfloat16 or wider, within the bound.
A program may use at most 128 MiB of HBM per device.

v0:
```python
import jax
import jax.numpy as jnp
from jax import lax
from jax.sharding import PartitionSpec as P


def from_behind(block, axis, distance):
    devices = range(lax.axis_size(axis))
    route = [(i - distance, i) for i in devices if i - distance in devices]
    return lax.ppermute(block, axis, route)


def depthwise(signal, kernel):
    channels = signal.shape[1]
    result = lax.conv_general_dilated(
        signal.astype(jnp.float32)[None],
        kernel.astype(jnp.float32)[:, None, :],
        (1,),
        "VALID",
        dimension_numbers=("NWC", "WIO", "NWC"),
        feature_group_count=channels,
        precision=lax.Precision.HIGHEST,
    )
    return result[0]


def causal_sum(extended, taps, out_rows):
    return depthwise(extended[: out_rows + taps.shape[0] - 1], taps[::-1])


def anticausal_sum(extended, taps, out_rows):
    return depthwise(extended[: out_rows + taps.shape[0] - 1], taps)


def lag_sums(left_rows, extended):
    return depthwise(extended, left_rows)[::-1]


def per_device(inputs, feat_weight, filter_taps, upstream):
    inputs_here = inputs[0]
    grad_here = upstream[0]
    tokens_here = inputs_here.shape[0]
    channels = grad_here.shape[1]
    feat_full, taps_full = (
        lax.all_gather(feat_weight, "dp", axis=1, tiled=True),
        lax.all_gather(filter_taps, "dp", axis=1, tiled=True),
    )
    feat_reach = feat_full.shape[0] - 1
    filt_reach = taps_full.shape[0] - 1
    scale = (lax.axis_size("dp") * lax.axis_size("ctx") * tokens_here) ** (-0.5)
    after_grad, after_inputs = from_behind(
        (grad_here[:filt_reach], inputs_here[:filt_reach, :channels]), "ctx", -1
    )
    before_inputs = from_behind(inputs_here[tokens_here - feat_reach :], "ctx", 1)
    inputs_ext = jnp.concatenate([before_inputs, inputs_here], 0)
    featured = causal_sum(inputs_ext, feat_full, tokens_here)
    query = featured[:, :channels]
    key_part = featured[:, channels : 2 * channels]
    value_part = featured[:, 2 * channels :]
    mixed = (key_part * value_part).astype(jnp.bfloat16)
    before_mixed = from_behind(mixed[tokens_here - filt_reach :], "ctx", 1)
    mixed_ext = jnp.concatenate([before_mixed, mixed], 0)
    conv_out = causal_sum(mixed_ext, taps_full, tokens_here)
    grad_conv = (grad_here * query).astype(jnp.bfloat16)
    query_ext = jnp.concatenate(
        [inputs_here[tokens_here - feat_reach :, :channels], after_inputs], 0
    )
    after_query = causal_sum(query_ext, feat_full[:, :channels], filt_reach)
    grad_after = (after_grad * after_query).astype(jnp.bfloat16)
    grad_ext = jnp.concatenate([grad_conv, grad_after], 0)
    grad_mixed = anticausal_sum(grad_ext, taps_full, tokens_here)
    grad_feat = jnp.concatenate(
        [grad_here * conv_out, grad_mixed * value_part, grad_mixed * key_part], 1
    )
    filter_part = lag_sums(grad_conv, mixed_ext)
    feat_part = lag_sums(grad_feat, inputs_ext)
    filter_whole, feat_whole = lax.psum((filter_part, feat_part), "ctx")
    filter_summed, feat_summed = (
        lax.psum_scatter(filter_whole, "dp", scatter_dimension=1, tiled=True),
        lax.psum_scatter(feat_whole, "dp", scatter_dimension=1, tiled=True),
    )
    return (filter_summed * scale, feat_summed * scale)


def solution(mesh):
    placed = (P("dp", "ctx", None), P(None, "dp"), P(None, "dp"), P("dp", "ctx", None))
    return jax.shard_map(
        per_device,
        mesh=mesh,
        in_specs=placed,
        out_specs=(P(None, "dp"), P(None, "dp")),
        check_vma=False,
    )
```

profile of v0, /device:TPU:26, one launch (start us, length us, event | category | flops | bytes accessed | tf_op | source)
XLA Modules:
  0.0 430.9 jit_solution(4820415927068143352)
XLA Ops:
  7.2 1.1 slice_bitcast_fusion.3
  8.3 3.4 collective-permute-start
  11.7 2.3 slice.55
  14.0 2.4 collective-permute-start.3
  16.5 1.1 slice_bitcast_fusion.2
  17.5 4.2 collective-permute-start.2
  21.9 0.9 slice.54
  22.7 2.1 all_gather.6
  24.8 28.5 %rev.15 = f32[7,12288]{1,0:T(8,128)} reverse(f32[7,12288]{1,0:T(8,128)S(1)} %all_gather.6), dimensions={0} | reverse | bytes 688128 | tf_op jit(solution)/shard_map/rev | solution.py:28
  53.3 0.7 rev.18
  54.1 2.7 maximum_bitcast_fusion.1
  56.8 1.7 copy-done.1
  58.9 3.5 reshape.10
  62.5 4.3 copy.14
  67.0 0.7 copy-done.12
  67.7 3.5 convolution_select_fusion
  71.2 8.0 %copy.16 = f32[8,17,12288]{2,1,0:T(8,128)} copy(f32[8,17,12288]{2,0,1:T(8,128)S(1)} %convolution_select_fusion) | data formatting | bytes 13369344 | tf_op jit(solution)/shard_map/conv_general_dilated | solution.py:15
  79.2 7.3 %reshape.14 = f32[1,136,12288]{2,1,0:T(8,128)} reshape(f32[8,17,12288]{2,1,0:T(8,128)} %copy.16) | data formatting | bytes 13369344 | tf_op jit(solution)/shard_map/conv_general_dilated | solution.py:15
  86.4 3.3 slice_bitcast_fusion
  89.8 1.4 fusion.18
  91.1 2.3 maximum_bitcast_fusion.4
  94.0 0.7 copy.22
  94.8 1.2 convolution_select_fusion.1
  95.9 1.3 copy.24
  97.3 1.7 reshape.21
  99.0 2.2 fusion.20
  101.4 4.1 broadcast_in_dim.40
  105.5 23.6 %fusion.10 = f32[1,128,4096]{2,0,1:T(1,128)S(1)} fusion(f32[128,1,4096]{2,1,0:T(1,128)S(1)} %broadcast_in_dim.40, bf16[1,255,4096]{2,1,0:T(8,128)(2,1)S(1)} %maximum_bitcast_fusion.3), kind=kOutput, calls=%fused_computation.14 | convolution fusion | flops 805306368 | bytes 6283264 | tf_op jit(solution)/shard_map/conv_general_dilated | solution.py:15
  129.2 4.0 bitcast_multiply_fusion.1
  133.1 1.2 slice.52
  134.4 2.5 collective-permute-start.1
  136.9 10.7 %rev.17 = f32[128,4096]{1,0:T(8,128)} reverse(f32[128,4096]{1,0:T(8,128)S(1)} %copy-done.6), dimensions={0} | reverse | bytes 4194304 | tf_op jit(solution)/shard_map/rev | solution.py:28
  147.6 14.2 %collective-permute-done.1 = bf16[127,4096]{1,0:T(8,128)(2,1)} collective-permute-done((bf16[127,4096]{1,0:T(8,128)(2,1)}, bf16[127,4096]{1,0:T(8,128)(2,1)}, u32[]{:S(2)}, u32[]{:S(2)}) %collective-permute-start.1) | collective-permute-done | bytes 1040416 | tf_op jit(solution)/shard_map/ppermute | solution.py:10
  161.8 1.5 maximum_bitcast_fusion.2
  163.3 23.9 %fusion.12 = f32[1,128,4096]{2,0,1:T(1,128)S(1)} fusion(bf16[1,255,4096]{2,1,0:T(8,128)(2,1)S(1)} %maximum_bitcast_fusion.2, f32[128,1,4096]{2,0,1:T(8,128)S(1)} %bitcast.56), kind=kOutput, calls=%fused_computation.17 | convolution fusion | flops 805306368 | bytes 6283264 | tf_op jit(solution)/shard_map/conv_general_dilated | solution.py:15
  187.2 1.8 convert_multiply_fusion
  189.4 0.6 maximum_bitcast_fusion
  190.0 1.4 copy-done.2
  191.4 14.8 %fusion.1 = f32[1,7,12288]{2,0,1:T(1,128)S(1)} fusion(bf16[1,134,12288]{2,1,0:T(8,128)(2,1)S(1)} %copy-done.2, f32[128,1,12288]{2,0,1:T(8,128)S(1)} %maximum_bitcast_fusion), kind=kOutput, calls=%fused_computation.3 | convolution fusion | flops 132120576 | bytes 9928704 | tf_op jit(solution)/shard_map/conv_general_dilated | solution.py:15
  206.2 1.0 copy.56
  207.1 41.6 %rev.19 = f32[7,12288]{1,0:T(8,128)} reverse(f32[7,12288]{1,0:T(8,128)} %bitcast.57), dimensions={0} | reverse | bytes 688128 | tf_op jit(solution)/shard_map/rev | solution.py:36
  248.8 30.1 %fusion.14 = f32[1,128,4096]{2,0,1:T(1,128)S(1)} fusion(bf16[1,255,4096]{2,1,0:T(8,128)(2,1)S(1)} %maximum_bitcast_fusion.2, bf16[128,1,4096]{2,0,1:T(8,128)(2,1)S(1)} %bitcast.55), kind=kOutput, calls=%fused_computation.19 | convolution fusion | flops 134217728 | bytes 5234688 | tf_op jit(solution)/shard_map/conv_general_dilated | solution.py:15
  278.9 1.6 copy.55
  280.5 10.5 %rev.16 = f32[128,4096]{1,0:T(8,128)} reverse(f32[128,4096]{1,0:T(8,128)S(1)} %bitcast.51), dimensions={0} | reverse | bytes 4194304 | tf_op jit(solution)/shard_map/rev | solution.py:36
  291.1 11.2 %reduce-scatter.3.cloned.1.call-done = f32[128,2048]{1,0:T(8,128)} async-done(((f32[128,4096]{1,0:T(8,128)}), f32[128,2048]{1,0:T(8,128)}) %reduce-scatter.3.cloned.1.call-update) | async-done | bytes 1048592 | tf_op jit(solution)/shard_map/reduce_scatter | solution.py:79
  302.3 119.0 %all-reduce.3.cloned.1.call-done = (f32[128,2048]{1,0:T(8,128)}, f32[7,6144]{1,0:T(8,128)}) async-done(((f32[128,2048]{1,0:T(8,128)}, f32[7,6144]{1,0:T(8,128)}), (f32[128,2048]{1,0:T(8,128)}, f32[7,6144]{1,0:T(8,128)})) %all-reduce.3.cloned.1.call-update) | async-done | bytes 1220624 | tf_op jit(solution)/shard_map/psum | solution.py:77
  421.3 2.3 broadcast_multiply_fusion
  423.7 0.7 broadcast_multiply_fusion.1
  (56 shorter events, 2.1 us)
Async XLA Ops:
  7.2 9.3 %copy-start.3 = (bf16[1,128,4096]{2,1,0:T(8,128)(2,1)S(1)}, bf16[1,128,4096]{2,1,0:T(8,128)(2,1)}, u32[]{:S(2)}) copy-start(bf16[1,128,4096]{2,1,0:T(8,128)(2,1)} %param.7) | copy-start | bytes 3145732
  7.2 94.2 %all-gather.2.cloned.1.call-start = ((), (), s32[]{:S(2)}) async-start(), calls=%async_computation.2 | async-start | bytes 3145728 | tf_op jit(solution)/shard_map/all_gather | solution.py:46
  8.3 45.8 %collective-permute-start = (bf16[6,12288]{1,0:T(8,128)(2,1)S(1)}, bf16[6,12288]{1,0:T(8,128)(2,1)S(1)}, u32[]{:S(2)}, u32[]{:S(2)}) collective-permute-start(bf16[6,12288]{1,0:T(8,128)(2,1)S(1)} %slice_bitcast_fusion.3), channel_id=1, source_target_pairs={{0,2},{2,4},{4,6},{6,8},{8,10},{10,12},{12,14},{14,16},{16,18},{18... | collective-permute-start | bytes 442376 | tf_op jit(solution)/shard_map/ppermute | solution.py:10
  11.7 11.0 %copy-start.14 = (f32[7,6144]{1,0:T(8,128)S(1)}, f32[7,6144]{1,0:T(8,128)}, u32[]{:S(2)}) copy-start(f32[7,6144]{1,0:T(8,128)} %param.5) | copy-start | bytes 516100
  14.0 77.1 %collective-permute-start.3 = (bf16[127,4096]{1,0:T(8,128)(2,1)}, bf16[127,4096]{1,0:T(8,128)(2,1)}, u32[]{:S(2)}, u32[]{:S(2)}) collective-permute-start(bf16[127,4096]{1,0:T(8,128)(2,1)} %slice.55), channel_id=1, source_target_pairs={{2,0},{4,2},{6,4},{8,6},{10,8},{12,10},{14,12},{16,14},{18,16},{20... | collective-permute-start | bytes 3121160 | tf_op jit(solution)/shard_map/ppermute | solution.py:10
  17.5 81.5 %collective-permute-start.2 = (bf16[127,4096]{1,0:T(8,128)(2,1)}, bf16[127,4096]{1,0:T(8,128)(2,1)}, u32[]{:S(2)}, u32[]{:S(2)}) collective-permute-start(bf16[127,4096]{1,0:T(8,128)(2,1)} %slice_bitcast_fusion.2), channel_id=1, source_target_pairs={{2,0},{4,2},{6,4},{8,6},{10,8},{12,10},{14,12},{16,14},{18,16},{20... | collective-permute-start | bytes 3121160 | tf_op jit(solution)/shard_map/ppermute | solution.py:10
  21.8 269.3 %reduce-scatter.5.cloned.1.call-start = ((), (), s32[]{:S(2)}) async-start(), calls=%async_computation.4 | async-start | bytes 589824 | tf_op jit(solution)/shard_map/reduce_scatter | solution.py:80
  56.8 1.7 copy-start.1
  66.7 1.0 copy-start.12
  66.7 1.0 copy-start.16
  86.4 3.3 copy-start.4
  89.8 3.7 copy-start
  94.0 0.8 copy-start.15
  99.0 2.2 copy-start.9
  101.4 27.8 %slice-start = ((s8[6291456]{0:T(1024)(128)(4,1)}), s8[2097152]{0:T(1024)(128)(4,1)S(1)}, s32[]{:S(2)}) async-start(s8[6291456]{0:T(1024)(128)(4,1)} %bitcast.49), calls=%async_computation.6 | async-start | bytes 4194304
  105.5 23.6 %slice-start.1 = ((s8[6291456]{0:T(1024)(128)(4,1)}), s8[4194304]{0:T(1024)(128)(4,1)S(1)}, s32[]{:S(2)}) async-start(s8[6291456]{0:T(1024)(128)(4,1)} %bitcast.49), calls=%async_computation.7 | async-start | bytes 8388608
  133.1 3.7 copy-start.6
  134.4 27.4 %collective-permute-start.1 = (bf16[127,4096]{1,0:T(8,128)(2,1)}, bf16[127,4096]{1,0:T(8,128)(2,1)}, u32[]{:S(2)}, u32[]{:S(2)}) collective-permute-start(bf16[127,4096]{1,0:T(8,128)(2,1)} %slice.52), channel_id=1, source_target_pairs={{0,2},{2,4},{4,6},{6,8},{8,10},{10,12},{12,14},{14,16},{16,18},{18... | collective-permute-start | bytes 3121160 | tf_op jit(solution)/shard_map/ppermute | solution.py:10
  147.6 15.7 %copy-start.11 = (f32[128,4096]{1,0:T(8,128)S(1)}, f32[128,4096]{1,0:T(8,128)}, u32[]{:S(2)}) copy-start(f32[128,4096]{1,0:T(8,128)} %rev.17) | copy-start | bytes 6291460
  163.3 23.9 %copy-start.5 = (bf16[1,128,4096]{2,1,0:T(8,128)(2,1)S(1)}, bf16[1,128,4096]{2,1,0:T(8,128)(2,1)}, u32[]{:S(2)}) copy-start(bf16[1,128,4096]{2,1,0:T(8,128)(2,1)} %param.7) | copy-start | bytes 3145732
  187.2 1.9 copy-start.7
  187.2 2.2 copy-start.8
  189.4 1.9 copy-start.2
  191.4 57.4 %copy-start.10 = (bf16[128,4096]{1,0:T(8,128)(2,1)S(1)}, bf16[128,4096]{1,0:T(8,128)(2,1)}, u32[]{:S(2)}) copy-start(bf16[128,4096]{1,0:T(8,128)(2,1)} %fusion.18) | copy-start | bytes 3145732
  248.7 53.6 %reduce-scatter.3.cloned.1.call-start = ((), (), s32[]{:S(2)}) async-start(), calls=%async_computation.3 | async-start | bytes 3145728 | tf_op jit(solution)/shard_map/reduce_scatter | solution.py:79
  291.0 130.3 %all-reduce.3.cloned.1.call-start = ((), (), s32[]{:S(2)}) async-start(), calls=%async_computation.5 | async-start | bytes 2490368 | tf_op jit(solution)/shard_map/psum | solution.py:77
  421.3 2.3 copy-start.13
Sparse Core Ops, SparseCore 0:
  21.9 11.8 all-gather.1
  248.8 9.0 reduce-scatter.4
  291.2 11.0 reduce-scatter.2
  307.5 113.7 all-reduce.2
where the time goes:
time: 437 us; the launch traced here: 431 us
  waiting for transfers between devices  144 us (33%)
  local copies, waits for them, and re-layouts  141 us (32%)
  matrix products  97 us (22%)
  other arithmetic  19.7 us (5%)
  between operations  14.2 us (3%)
  starting transfers between devices  12.7 us (3%)
    psum x1, waiting for transfers between devices, per_device(): filter_whole, feat_whole = lax.psum((filter_part, feat_part), 'ctx')  119 us
    conv_general_dilated x6, matrix products, depthwise(): lax.conv_general_dilated(signal.astype(jnp.float32)[None], kernel.astype(...  97 us
    rev x2, local copies, waits for them, and re-layouts, lag_sums(): return depthwise(extended, left_rows)[::-1]  52.1 us
    rev x3, local copies, waits for them, and re-layouts, causal_sum(): return depthwise(extended[:out_rows + taps.shape[0] - 1], taps[::-1])  40 us
    conv_general_dilated x10, local copies, waits for them, and re-layouts, depthwise(): lax.conv_general_dilated(signal.astype(jnp.float32)[None], kernel.astype(...  27.5 us
    ppermute x4, waiting for transfers between devices, from_behind(): return lax.ppermute(block, axis, route)  14.2 us
    ppermute x4, starting transfers between devices, from_behind(): return lax.ppermute(block, axis, route)  12.6 us
    reduce_scatter x1, waiting for transfers between devices, per_device(): lax.psum_scatter(filter_whole, 'dp', scatter_dimension=1, tiled=True)  11.2 us
  transfers between devices with their start and end apart: 8, of which 3 were waited for; matrix products, arithmetic and copies ran while one was open for 30% of the time, Pallas kernels for 0%

commit v1 on v0

v1 whole, which is shorter than its diff:
```python
import functools

import jax
import jax.numpy as jnp
import numpy as np
from jax import lax
from jax.experimental import pallas as pl
from jax.experimental.pallas import tpu as pltpu
from jax.sharding import PartitionSpec as P

PAD = 8
F32 = jnp.float32
BF16 = jnp.bfloat16


def from_behind(block, axis, distance):
    devices = range(lax.axis_size(axis))
    route = [(i - distance, i) for i in devices if i - distance in devices]
    return lax.ppermute(block, axis, route)


def two_parts(matrix):
    high = matrix.astype(BF16)
    low = (matrix - high.astype(np.float64)).astype(BF16)
    return high, low


def transforms(rows, taps):
    size = rows + taps
    half = size // 2
    angle = 2 * np.pi * np.outer(np.arange(half), np.arange(size)) / size
    cosines = np.cos(angle)
    sines = -np.sin(angle)
    sines[0] = np.cos(np.pi * np.arange(size))
    forward = np.concatenate([cosines, sines], 0)
    weight = np.full((size, 1), 2.0 / size)
    weight[0] = weight[half] = 1.0 / size
    backward = (forward * weight).T
    f_high, f_low = two_parts(forward)
    b_high, b_low = two_parts(backward)
    cat = lambda *parts: np.concatenate(parts, 1)
    return (
        cat(f_high[:, :rows], f_low[:, :rows]),
        cat(f_high[:, :taps], f_low[:, :taps], f_high[:, :taps]),
        cat(f_high, f_low),
        cat(b_high, b_low),
    )


def dot(a, b):
    return jnp.dot(a, b, preferred_element_type=F32)


def chunk_terms(q_ext, k_ext, v_ext, up_ext, taps, weights, mats, rows, reach):
    to_mixed, to_taps, to_grad, back = mats
    size = up_ext.shape[0]
    half = size // 2

    def featured(ext, w, out_rows):
        total = w[0:1] * ext[PAD : PAD + out_rows, :]
        for j in range(1, reach):
            total += w[j : j + 1] * ext[PAD - j : PAD - j + out_rows, :]
        return total

    def lagged(grad, ext, out_rows):
        sums = [
            jnp.sum(grad * ext[PAD - j : PAD - j + out_rows, :], 0, keepdims=True)
            for j in range(reach)
        ]
        sums += [jnp.zeros_like(sums[0])] * (PAD - reach)
        return jnp.concatenate(sums, 0)

    key_part = featured(k_ext, weights[1], rows)
    value_part = featured(v_ext, weights[2], rows)
    mixed = (key_part * value_part).astype(BF16)
    m_hat = dot(to_mixed[...], jnp.concatenate([mixed, mixed], 0))
    taps_high = taps.astype(BF16)
    taps_low = (taps - taps_high.astype(F32)).astype(BF16)
    t_hat = dot(to_taps[...], jnp.concatenate([taps_high, taps_high, taps_low], 0))
    query = featured(q_ext, weights[0], size)
    grad_conv = (up_ext[...].astype(F32) * query).astype(BF16)
    g_hat = dot(to_grad[...], jnp.concatenate([grad_conv, grad_conv], 0))

    m_re, m_im = m_hat[:half], m_hat[half:]
    t_re, t_im = t_hat[:half], t_hat[half:]
    g_re, g_im = g_hat[:half], g_hat[half:]
    first = lax.broadcasted_iota(jnp.int32, m_re.shape, 0) == 0
    t_imz = jnp.where(first, 0.0, t_im)
    t_ren = jnp.where(first, t_im, t_re)
    m_imz = jnp.where(first, 0.0, m_im)
    m_ren = jnp.where(first, m_im, m_re)

    def inverse(re, im, out_rows):
        re, im = re.astype(BF16), im.astype(BF16)
        return dot(back[:out_rows, :], jnp.concatenate([re, im, re, im], 0))

    conv_out = inverse(
        m_re * t_re - m_im * t_imz, m_re * t_imz + m_im * t_ren, size
    )
    grad_mixed = inverse(
        g_re * t_re + g_im * t_imz, g_im * t_ren - g_re * t_imz, rows
    )
    filter_part = inverse(
        g_re * m_re + g_im * m_imz, g_im * m_ren - g_re * m_imz, taps.shape[0]
    )
    return (
        filter_part,
        lagged(up_ext[...].astype(F32) * conv_out, q_ext, size),
        lagged(grad_mixed * value_part, k_ext, rows),
        lagged(grad_mixed * key_part, v_ext, rows),
    )


def local_kernel(
    reach, xq, xk, xv, pq, pk, pv, nq, up, nup, taps, wq, wk, wv, m0, m1, m2, m3,
    filt, fq, fk, fv, q_ext, k_ext, v_ext, up_ext,
):
    rows = xq.shape[0]
    size = up_ext.shape[0]
    for ext, prev, block in ((q_ext, pq, xq), (k_ext, pk, xk), (v_ext, pv, xv)):
        ext[0:PAD, :] = prev[...].astype(F32)
        ext[PAD : PAD + rows, :] = block[...].astype(F32)
    q_ext[PAD + rows : PAD + size, :] = nq[...].astype(F32)
    up_ext[0:rows, :] = up[...]
    up_ext[rows:size, :] = nup[...]
    filt[...], fq[...], fk[...], fv[...] = chunk_terms(
        q_ext, k_ext, v_ext, up_ext, taps[...], (wq[...], wk[...], wv[...]),
        (m0, m1, m2, m3), rows, reach,
    )


def per_device(inputs, feat_weight, filter_taps, upstream):
    inputs_here = inputs[0]
    grad_here = upstream[0]
    rows = inputs_here.shape[0]
    channels = grad_here.shape[1]
    filt_rows = filter_taps.shape[0]
    reach = feat_weight.shape[0]
    scale = (lax.axis_size("dp") * lax.axis_size("ctx") * rows) ** (-0.5)
    feat_full, taps_full = (
        lax.all_gather(feat_weight, "dp", axis=1, tiled=True),
        lax.all_gather(filter_taps, "dp", axis=1, tiled=True),
    )
    next_grad, next_query = from_behind(
        (grad_here[:filt_rows], inputs_here[:filt_rows, :channels]), "ctx", -1
    )
    before = from_behind(inputs_here[rows - PAD :], "ctx", 1)
    weights = jnp.concatenate(
        [feat_full, jnp.zeros((PAD - reach, feat_full.shape[1]), F32)], 0
    )
    mats = [jnp.asarray(m) for m in transforms(rows, filt_rows)]
    width = 256
    steps = channels // width
    size = rows + filt_rows
    part = lambda r, group: pl.BlockSpec((r, width), lambda i: (0, i + group * steps))
    whole = lambda m: pl.BlockSpec(m.shape, lambda i: (0, 0))
    out = lambda r: jax.ShapeDtypeStruct((r, channels), F32)
    filter_part, feat_q, feat_k, feat_v = pl.pallas_call(
        functools.partial(local_kernel, reach),
        grid=(steps,),
        out_shape=[out(filt_rows), out(PAD), out(PAD), out(PAD)],
        in_specs=[part(rows, g) for g in range(3)]
        + [part(PAD, g) for g in range(3)]
        + [part(filt_rows, 0), part(rows, 0), part(filt_rows, 0), part(filt_rows, 0)]
        + [part(PAD, g) for g in range(3)]
        + [whole(m) for m in mats],
        out_specs=[part(filt_rows, 0)] + [part(PAD, 0)] * 3,
        scratch_shapes=[
            pltpu.VMEM((PAD + size, width), F32),
            pltpu.VMEM((PAD + rows, width), F32),
            pltpu.VMEM((PAD + rows, width), F32),
            pltpu.VMEM((size, width), BF16),
        ],
    )(
        inputs_here, inputs_here, inputs_here, before, before, before, next_query,
        grad_here, next_grad, taps_full, weights, weights, weights, *mats,
    )
    feat_part = jnp.concatenate([feat_q, feat_k, feat_v], 1)[:reach]
    filter_summed, feat_summed = (
        lax.psum_scatter(filter_part, "dp", scatter_dimension=1, tiled=True),
        lax.psum_scatter(feat_part, "dp", scatter_dimension=1, tiled=True),
    )
    filter_whole, feat_whole = lax.psum((filter_summed, feat_summed), "ctx")
    return (filter_whole * scale, feat_whole * scale)


def solution(mesh):
    placed = (P("dp", "ctx", None), P(None, "dp"), P(None, "dp"), P("dp", "ctx", None))
    return jax.shard_map(
        per_device,
        mesh=mesh,
        in_specs=placed,
        out_specs=(P(None, "dp"), P(None, "dp")),
        check_vma=False,
    )
```

time: 437 us -> 249 us (0.57)
  local copies, waits for them, and re-layouts: 141 us -> 4.4 us
  matrix products: 97 us -> 0 us
  waiting for transfers between devices: 144 us -> 182 us
  Pallas kernels: 0 us -> 27.3 us
  other arithmetic: 19.7 us -> 5.71 us
    conv_general_dilated x6 -> x0, matrix products: 97 us -> none  [depthwise(): lax.conv_general_dilated(signal.astype(jnp.float32)[None], kernel.astype(...]
    rev x5 -> x0, local copies, waits for them, and re-layouts: 92 us -> none  [the longest x2 52.1 us: lag_sums(): return depthwise(extended, left_rows)[::-1]]
    conv_general_dilated x10 -> x0, local copies, waits for them, and re-layouts: 27.5 us -> none  [depthwise(): lax.conv_general_dilated(signal.astype(jnp.float32)[None], kernel.astype(...]
    pallas_call x0 -> x1, Pallas kernels: none -> 27.3 us  [per_device(): pl.pallas_call(functools.partial(local_kernel, reach), grid=(steps,), out...]
    ppermute x4 -> x3, waiting for transfers between devices: 14.2 us -> 38.5 us  [from_behind(): return lax.ppermute(block, axis, route)]
    reduce_scatter x2, waiting for transfers between devices: 11.2 us -> 23.5 us  [the longest x1 13.2 us: per_device(): lax.psum_scatter(filter_part, 'dp', scatter_dimension=1, tiled=True)]
    broadcast_in_dim x5 -> x0, other arithmetic: 7.28 us -> none  [the longest x4 6.71 us: depthwise(): signal.astype(jnp.float32)[None]]
    unnamed x40 -> x10, local copies, waits for them, and re-layouts: 6.78 us -> 1.34 us
  transfers between devices with their start and end apart: 8 -> 7, of which waited for: 3 -> 4; matrix products, arithmetic and copies ran while one was open for 30% -> 1% of each run, Pallas kernels for 0% -> 0%
where the time goes in v1:
time: 249 us; the launch traced here: 245 us
  waiting for transfers between devices  182 us (73%)
  Pallas kernels  27.3 us (11%)
  between operations  13.8 us (6%)
  starting transfers between devices  9.31 us (4%)
  other arithmetic  5.71 us (2%)
  local copies, waits for them, and re-layouts  4.4 us (2%)
    psum x1, waiting for transfers between devices, per_device(): filter_whole, feat_whole = lax.psum((filter_summed, feat_summed), 'ctx')  119 us
    ppermute x3, waiting for transfers between devices, from_behind(): return lax.ppermute(block, axis, route)  38.5 us
    pallas_call x1, Pallas kernels, per_device(): pl.pallas_call(functools.partial(local_kernel, reach), grid=(steps,), out...  27.3 us
    reduce_scatter x1, waiting for transfers between devices, per_device(): lax.psum_scatter(filter_part, 'dp', scatter_dimension=1, tiled=True)  13.2 us
    reduce_scatter x1, waiting for transfers between devices, per_device(): lax.psum_scatter(feat_part, 'dp', scatter_dimension=1, tiled=True)  10.2 us
    ppermute x3, starting transfers between devices, from_behind(): return lax.ppermute(block, axis, route)  9.15 us
  transfers between devices with their start and end apart: 7, of which 4 were waited for; matrix products, arithmetic and copies ran while one was open for 1% of the time, Pallas kernels for 0%

profile of v1, /device:TPU:26, one launch (start us, length us, event | category | flops | bytes accessed | tf_op | source)
XLA Modules:
  0.0 245.0 jit_solution(5911245310880562259)
XLA Ops:
  7.2 0.0 copy-start.1
  7.2 0.0 copy-start.4
  7.2 0.0 all-gather.2.cloned.1.call-start
  7.2 0.7 all-gather.2.cloned.1.call-update
  7.9 0.0 reduce-scatter.5.cloned.1.call-start
  8.0 1.3 slice.16
  9.3 2.4 collective-permute-start.1
  11.7 0.0 copy-done.1
  11.7 4.2 %collective-permute-start.2 = (bf16[128,4096]{1,0:T(8,128)(2,1)S(1)}, bf16[128,4096]{1,0:T(8,128)(2,1)S(1)}, u32[]{:S(2)}, u32[]{:S(2)}) collective-permute-start(bf16[128,4096]{1,0:T(8,128)(2,1)S(1)} %bitcast.9), channel_id=1, source_target_pairs={{2,0},{4,2},{6,4},{8,6},{10,8},{12,10},{14,12},{16,14},{18,16},{20... | collective-permute-start | bytes 3145736 | tf_op jit(solution)/shard_map/ppermute | solution.py:19
  16.0 1.0 slice_bitcast_fusion
  17.0 2.5 %collective-permute-start = (bf16[8,12288]{1,0:T(8,128)(2,1)S(1)}, bf16[8,12288]{1,0:T(8,128)(2,1)S(1)}, u32[]{:S(2)}, u32[]{:S(2)}) collective-permute-start(bf16[8,12288]{1,0:T(8,128)(2,1)S(1)} %slice_bitcast_fusion), channel_id=1, source_target_pairs={{0,2},{2,4},{4,6},{6,8},{8,10},{10,12},{12,14},{14,16},{16,18},{18... | collective-permute-start | bytes 589832 | tf_op jit(solution)/shard_map/ppermute | solution.py:19
  19.4 0.0 copy-done.4
  19.4 2.1 all_gather.7
  21.5 0.8 concatenate.6.wq.wk.wv
  22.3 38.5 %collective-permute-done.pq.pk.pv = bf16[8,12288]{1,0:T(8,128)(2,1)S(1)} collective-permute-done((bf16[8,12288]{1,0:T(8,128)(2,1)S(1)}, bf16[8,12288]{1,0:T(8,128)(2,1)S(1)}, u32[]{:S(2)}, u32[]{:S(2)}) %collective-permute-start) | collective-permute-done | bytes 196640 | tf_op jit(solution)/shard_map/ppermute | solution.py:19
  60.8 0.0 copy-start
  60.8 0.0 collective-permute-done.1.nq
  60.8 0.0 copy-start.2
  60.8 0.0 collective-permute-done.2.nup
  60.8 0.0 copy-start.3
  60.8 0.0 all-gather.2.cloned.1.call-done.taps
  60.8 0.6 copy-done
  61.5 0.4 copy-done.2
  61.8 0.3 copy-done.3
  62.2 27.3 %shard_map.95 = (f32[128,4096]{1,0:T(8,128)}, f32[8,4096]{1,0:T(8,128)}, f32[8,4096]{1,0:T(8,128)}, f32[8,4096]{1,0:T(8,128)}) custom-call(bf16[128,12288]{1,0:T(8,128)(2,1)} %bitcast.5, bf16[128,12288]{1,0:T(8,128)(2,1)} %bitcast.6, bf16[128,12288]{1,0:T(8,128)(2,1)} %bitcast.7, bf16[8,12288]{1,0:T(8,128)(2,1)} %copy-done, bf16[8,12288]{1,0:T(8,128)(2,1)} %copy-done, ...), custom_call_target="tpu_custom_call" | custom-call | tf_op jit(solution)/shard_map/pallas_call | solution.py:158
  89.5 1.8 pad_maximum_fusion
  91.3 0.0 reduce-scatter.5.cloned.1.call-update
  91.3 0.0 reduce-scatter.3.cloned.1.call-start
  91.4 0.7 reduce-scatter.3.cloned.1.call-update
  92.0 0.0 all-reduce.4.cloned.1.call-start
  92.1 10.2 %reduce-scatter.5.cloned.1.call-done = f32[7,6144]{1,0:T(8,128)} async-done(((f32[7,12288]{1,0:T(8,128)}), f32[7,6144]{1,0:T(8,128)}) %reduce-scatter.5.cloned.1.call-update) | async-done | bytes 172048 | tf_op jit(solution)/shard_map/reduce_scatter | solution.py:181
  102.3 13.2 %reduce-scatter.3.cloned.1.call-done = f32[128,2048]{1,0:T(8,128)} async-done(((f32[128,4096]{1,0:T(8,128)}), f32[128,2048]{1,0:T(8,128)}) %reduce-scatter.3.cloned.1.call-update) | async-done | bytes 1048592 | tf_op jit(solution)/shard_map/reduce_scatter | solution.py:180
  115.6 0.0 all-reduce.4.cloned.1.call-update
  115.6 119.0 %all-reduce.4.cloned.1.call-done = (f32[128,2048]{1,0:T(8,128)}, f32[7,6144]{1,0:T(8,128)}) async-done(((f32[128,2048]{1,0:T(8,128)}, f32[7,6144]{1,0:T(8,128)}), (f32[128,2048]{1,0:T(8,128)}, f32[7,6144]{1,0:T(8,128)})) %all-reduce.4.cloned.1.call-update) | async-done | bytes 1220624 | tf_op jit(solution)/shard_map/psum | solution.py:183
  234.6 2.3 broadcast_multiply_fusion
  236.9 1.6 broadcast_multiply_fusion.1
Async XLA Ops:
  7.2 4.6 %copy-start.1 = (bf16[1,128,4096]{2,1,0:T(8,128)(2,1)S(1)}, bf16[1,128,4096]{2,1,0:T(8,128)(2,1)}, u32[]{:S(2)}) copy-start(bf16[1,128,4096]{2,1,0:T(8,128)(2,1)} %param.11) | copy-start | bytes 3145732
  7.2 12.3 %copy-start.4 = (f32[7,6144]{1,0:T(8,128)S(1)}, f32[7,6144]{1,0:T(8,128)}, u32[]{:S(2)}) copy-start(f32[7,6144]{1,0:T(8,128)} %param.9) | copy-start | bytes 516100
  7.2 53.7 %all-gather.2.cloned.1.call-start = ((), (), s32[]{:S(2)}) async-start(), calls=%async_computation.2 | async-start | bytes 3145728 | tf_op jit(solution)/shard_map/all_gather | solution.py:142
  7.9 94.4 %reduce-scatter.5.cloned.1.call-start = ((), (), s32[]{:S(2)}) async-start(), calls=%async_computation.4 | async-start | bytes 589824 | tf_op jit(solution)/shard_map/reduce_scatter | solution.py:181
  9.3 51.5 %collective-permute-start.1 = (bf16[128,4096]{1,0:T(8,128)(2,1)S(1)}, bf16[128,4096]{1,0:T(8,128)(2,1)S(1)}, u32[]{:S(2)}, u32[]{:S(2)}) collective-permute-start(bf16[128,4096]{1,0:T(8,128)(2,1)S(1)} %slice.16), channel_id=1, source_target_pairs={{2,0},{4,2},{6,4},{8,6},{10,8},{12,10},{14,12},{16,14},{18,16},{20... | collective-permute-start | bytes 3145736 | tf_op jit(solution)/shard_map/ppermute | solution.py:19
  11.7 49.1 %collective-permute-start.2 = (bf16[128,4096]{1,0:T(8,128)(2,1)S(1)}, bf16[128,4096]{1,0:T(8,128)(2,1)S(1)}, u32[]{:S(2)}, u32[]{:S(2)}) collective-permute-start(bf16[128,4096]{1,0:T(8,128)(2,1)S(1)} %bitcast.9), channel_id=1, source_target_pairs={{2,0},{4,2},{6,4},{8,6},{10,8},{12,10},{14,12},{16,14},{18,16},{20... | collective-permute-start | bytes 3145736 | tf_op jit(solution)/shard_map/ppermute | solution.py:19
  17.0 43.8 %collective-permute-start = (bf16[8,12288]{1,0:T(8,128)(2,1)S(1)}, bf16[8,12288]{1,0:T(8,128)(2,1)S(1)}, u32[]{:S(2)}, u32[]{:S(2)}) collective-permute-start(bf16[8,12288]{1,0:T(8,128)(2,1)S(1)} %slice_bitcast_fusion), channel_id=1, source_target_pairs={{0,2},{2,4},{4,6},{6,8},{8,10},{10,12},{12,14},{14,16},{16,18},{18... | collective-permute-start | bytes 589832 | tf_op jit(solution)/shard_map/ppermute | solution.py:19
  60.8 0.7 copy-start
  60.8 1.0 copy-start.2
  60.8 1.4 copy-start.3
  91.3 24.3 %reduce-scatter.3.cloned.1.call-start = ((), (), s32[]{:S(2)}) async-start(), calls=%async_computation.3 | async-start | bytes 3145728 | tf_op jit(solution)/shard_map/reduce_scatter | solution.py:180
  92.0 142.5 %all-reduce.4.cloned.1.call-start = ((), (), s32[]{:S(2)}) async-start(), calls=%async_computation.5 | async-start | bytes 2490368 | tf_op jit(solution)/shard_map/psum | solution.py:183
Sparse Core Ops, SparseCore 0:
  9.5 12.0 all-gather.1
  91.4 10.8 reduce-scatter.4
  104.6 10.9 reduce-scatter.2
  120.8 113.7 all-reduce.3

commit v2 on v1

--- a/solution.py
+++ b/solution.py
@@ -129,7 +129,7 @@
     )
 
 
-def per_device(inputs, feat_weight, filter_taps, upstream):
+def by_collectives(inputs, feat_weight, filter_taps, upstream):
     inputs_here = inputs[0]
     grad_here = upstream[0]
     rows = inputs_here.shape[0]
@@ -184,6 +184,286 @@
     return (filter_whole * scale, feat_whole * scale)
 
 
+MESH = pl.DeviceIdType.MESH
+LANES = 128
+
+
+def fused_kernel(
+    reach, scale, x, up, tail, taps_here, w_here, m0, m1, m2, m3, filt_out, feat_out,
+    taps_all, w_all, prev, n_up, n_q, q_ext, k_ext, v_ext, up_ext,
+    stage, dp_got, rs_send, rs_got, gathered,
+    own_sem, swap_send, swap_got, tail_send, tail_got, halo_send, halo_got,
+    dp_send, dp_recv, rs_ssem, rs_rsem, ag_ssem, ag_rsem,
+):
+    n = lax.axis_size("ctx")
+    me, core = lax.axis_index("ctx"), lax.axis_index("dp")
+    rows, filt_rows = x.shape[0], taps_here.shape[0]
+    channels = up.shape[1]
+    half = channels // 2
+    feat_half = w_here.shape[1]
+    size = rows + filt_rows
+    packed = stage.shape[2]
+    partner = {"dp": 1 - core}
+
+    barrier = pltpu.get_barrier_semaphore()
+    pl.semaphore_signal(barrier, inc=1, device_id=partner, device_id_type=MESH)
+
+    @pl.loop(1, n)
+    def _(j):
+        pl.semaphore_signal(
+            barrier, inc=1, device_id={"ctx": lax.rem(me + j, n)}, device_id_type=MESH
+        )
+
+    def remote(src, dst, send, got, device):
+        return pltpu.make_async_remote_copy(
+            src_ref=src, dst_ref=dst, send_sem=send, recv_sem=got,
+            device_id=device, device_id_type=MESH,
+        )
+
+    def lanes_of(owner, piece):
+        return pl.ds(pl.multiple_of(owner * LANES + piece * half, LANES), LANES)
+
+    def swaps():
+        taps_side = pl.ds(pl.multiple_of(core * half, LANES), half)
+        feat_side = pl.ds(pl.multiple_of(core * feat_half, LANES), feat_half)
+        return (
+            remote(taps_here, taps_all.at[:, taps_side], swap_send.at[0], swap_got.at[0], partner),
+            remote(w_here, w_all.at[:, feat_side], swap_send.at[1], swap_got.at[1], partner),
+        ), (
+            pltpu.make_async_copy(taps_here, taps_all.at[:, taps_side], own_sem.at[0]),
+            pltpu.make_async_copy(w_here, w_all.at[:, feat_side], own_sem.at[1]),
+        )
+
+    def tail_copy():
+        return remote(tail, prev, tail_send, tail_got, {"ctx": lax.rem(me + 1, n)})
+
+    def halo_copies(i, owner):
+        target = {"ctx": lax.rem(me + n - 1, n)}
+        copies = []
+        for piece in range(2):
+            at = lanes_of(owner, piece)
+            for k, (src, dst) in enumerate(((up, n_up), (x, n_q))):
+                s = 2 * piece + k
+                copies.append(
+                    remote(
+                        src.at[pl.ds(0, filt_rows), at], dst.at[:, at],
+                        halo_send.at[i, s], halo_got.at[i, s], target,
+                    )
+                )
+        return copies
+
+    sent, kept = swaps()
+    for copy in kept:
+        copy.start()
+
+    @pl.when(me == 0)
+    def _():
+        prev[...] = jnp.zeros_like(prev)
+
+    @pl.when(me == n - 1)
+    def _():
+        n_up[...] = jnp.zeros_like(n_up)
+        n_q[...] = jnp.zeros_like(n_q)
+
+    pl.semaphore_wait(barrier, n)
+    for copy in sent:
+        copy.start()
+
+    @pl.when(me < n - 1)
+    def _():
+        tail_copy().start()
+
+    @pl.when(me > 0)
+    def _():
+        @pl.loop(0, n)
+        def _(i):
+            for copy in halo_copies(i, lax.rem(i + me, n)):
+                copy.start()
+
+    for copy in kept:
+        copy.wait()
+    for copy in sent:
+        copy.wait()
+
+    @pl.when(me > 0)
+    def _():
+        tail_copy().wait_recv()
+
+    def dp_copy(i):
+        return remote(
+            stage.at[i, 1 - core], dp_got.at[i], dp_send.at[i], dp_recv.at[i], partner
+        )
+
+    def rs_copy(i, owner):
+        return remote(
+            rs_send.at[i], rs_got.at[me], rs_ssem.at[i], rs_rsem.at[me], {"ctx": owner}
+        )
+
+    def owner_at(i):
+        return lax.rem(i + 1 + me, n)
+
+    def compute(i):
+        owner = owner_at(i)
+
+        @pl.when(me < n - 1)
+        def _():
+            for copy in halo_copies(i, owner):
+                copy.wait_recv()
+
+        def both(ref, group):
+            return jnp.concatenate(
+                [ref[:, pl.ds(pl.multiple_of(group * channels + p * half + owner * LANES, LANES), LANES)] for p in range(2)],
+                1,
+            )
+
+        for group, ext in enumerate((q_ext, k_ext, v_ext)):
+            ext[0:PAD, :] = both(prev, group).astype(F32)
+            ext[PAD : PAD + rows, :] = both(x, group).astype(F32)
+        q_ext[PAD + rows : PAD + size, :] = both(n_q, 0).astype(F32)
+        up_ext[0:rows, :] = both(up, 0)
+        up_ext[rows:size, :] = both(n_up, 0)
+        filt, feat_q, feat_k, feat_v = chunk_terms(
+            q_ext, k_ext, v_ext, up_ext, both(taps_all, 0),
+            [both(w_all, group) for group in range(3)],
+            (m0, m1, m2, m3), rows, reach,
+        )
+        a, b = slice(0, LANES), slice(LANES, 2 * LANES)
+        rest = [jnp.zeros((packed - filt_rows - 3 * PAD, LANES), F32)]
+        stage[i, 0] = jnp.concatenate(
+            [filt[:, a], feat_q[:, a], feat_q[:, b], feat_k[:, a]] + rest, 0
+        )
+        stage[i, 1] = jnp.concatenate(
+            [filt[:, b], feat_k[:, b], feat_v[:, a], feat_v[:, b]] + rest, 0
+        )
+        dp_copy(i).start()
+
+    def reduce_pair(i):
+        dp_copy(i).wait_recv()
+        return (stage[i, core] + dp_got[i]).astype(BF16)
+
+    def send_on(i):
+        rs_send[i] = reduce_pair(i)
+        rs_copy(i, owner_at(i)).start()
+
+    @pl.loop(0, n)
+    def _(i):
+        compute(i)
+
+        @pl.when(i > 0)
+        def _():
+            send_on(i - 1)
+
+    total = reduce_pair(n - 1).astype(F32)
+    for j in range(1, n):
+        src = lax.rem(me + j, n)
+        remote(
+            rs_send.at[0], rs_got.at[src], rs_ssem.at[0], rs_rsem.at[src], {"ctx": src}
+        ).wait_recv()
+        total += rs_got[src].astype(F32)
+    gathered[me] = total.astype(BF16)
+
+    def ag_copy(owner, target):
+        return remote(
+            gathered.at[owner], gathered.at[owner], ag_ssem.at[target], ag_rsem.at[owner],
+            {"ctx": target},
+        )
+
+    @pl.loop(1, n)
+    def _(j):
+        ag_copy(me, lax.rem(me + j, n)).start()
+
+    def unpack(owner):
+        value = gathered[owner].astype(F32) * scale
+        filt_out[:, pl.ds(pl.multiple_of(owner * LANES, LANES), LANES)] = value[:filt_rows]
+        for g in range(3):
+            low = filt_rows + g * PAD
+            at = pl.ds(pl.multiple_of(owner * LANES + g * half, LANES), LANES)
+            feat_out[:, at] = value[low : low + reach]
+
+    unpack(me)
+
+    @pl.loop(1, n)
+    def _(j):
+        src = lax.rem(me + j, n)
+        ag_copy(src, src).wait_recv()
+        unpack(src)
+
+    @pl.when(me < n - 1)
+    def _():
+        tail_copy().wait_send()
+
+    @pl.when(me > 0)
+    def _():
+        @pl.loop(0, n)
+        def _(i):
+            for copy in halo_copies(i, lax.rem(i + me, n)):
+                copy.wait_send()
+
+    @pl.loop(0, n)
+    def _(i):
+        dp_copy(i).wait_send()
+
+    @pl.loop(0, n - 1)
+    def _(i):
+        rs_copy(i, owner_at(i)).wait_send()
+
+    @pl.loop(1, n)
+    def _(j):
+        ag_copy(me, lax.rem(me + j, n)).wait_send()
+
+
+def fused(inputs, feat_weight, filter_taps, upstream):
+    x, up = inputs[0], upstream[0]
+    n = lax.axis_size("ctx")
+    rows, channels = up.shape
+    filt_rows, reach = filter_taps.shape[0], feat_weight.shape[0]
+    scale = (lax.axis_size("dp") * n * rows) ** (-0.5)
+    mats = [jnp.asarray(m) for m in transforms(rows, filt_rows)]
+    size = rows + filt_rows
+    width = 2 * LANES
+    packed = -(-(filt_rows + 3 * PAD) // 16) * 16
+    dma = lambda *shape: pltpu.SemaphoreType.DMA(shape)
+    return pl.pallas_call(
+        functools.partial(fused_kernel, reach, scale),
+        out_shape=[
+            jax.ShapeDtypeStruct(filter_taps.shape, F32),
+            jax.ShapeDtypeStruct(feat_weight.shape, F32),
+        ],
+        in_specs=[pl.BlockSpec(memory_space=pltpu.VMEM)] * 9,
+        out_specs=[pl.BlockSpec(memory_space=pltpu.VMEM)] * 2,
+        scratch_shapes=[
+            pltpu.VMEM((filt_rows, channels), F32),
+            pltpu.VMEM((reach, x.shape[1]), F32),
+            pltpu.VMEM((PAD, x.shape[1]), BF16),
+            pltpu.VMEM((filt_rows, channels), BF16),
+            pltpu.VMEM((filt_rows, channels), BF16),
+            pltpu.VMEM((PAD + size, width), F32),
+            pltpu.VMEM((PAD + rows, width), F32),
+            pltpu.VMEM((PAD + rows, width), F32),
+            pltpu.VMEM((size, width), BF16),
+            pltpu.VMEM((n, 2, packed, LANES), F32),
+            pltpu.VMEM((n, packed, LANES), F32),
+            pltpu.VMEM((n, packed, LANES), BF16),
+            pltpu.VMEM((n, packed, LANES), BF16),
+            pltpu.VMEM((n, packed, LANES), BF16),
+            dma(2), dma(2), dma(2),
+            pltpu.SemaphoreType.DMA, pltpu.SemaphoreType.DMA,
+            dma(n, 4), dma(n, 4),
+            dma(n), dma(n), dma(n), dma(n), dma(n), dma(n),
+        ],
+        compiler_params=pltpu.CompilerParams(
+            collective_id=0, has_side_effects=True, vmem_limit_bytes=60 * 2**20
+        ),
+    )(x, up, x[rows - PAD :], filter_taps, feat_weight, *mats)
+
+
+def per_device(inputs, feat_weight, filter_taps, upstream):
+    cut = 2 * lax.axis_size("ctx") * LANES
+    if lax.axis_size("dp") == 2 and upstream.shape[2] == cut:
+        return fused(inputs, feat_weight, filter_taps, upstream)
+    return by_collectives(inputs, feat_weight, filter_taps, upstream)
+
+
 def solution(mesh):
     placed = (P("dp", "ctx", None), P(None, "dp"), P(None, "dp"), P("dp", "ctx", None))
     return jax.shard_map(

time: 249 us -> 114 us (0.46); the launches traced: 245 us -> 113 us
  waiting for transfers between devices: 182 us -> 0 us
  Pallas kernels: 27.3 us -> 107 us
  between operations: 13.8 us -> 0.64 us
  starting transfers between devices: 9.31 us -> 0 us
  other arithmetic: 5.71 us -> 0 us
    psum x1 -> x0, waiting for transfers between devices: 119 us -> none  [per_device(): filter_whole, feat_whole = lax.psum((filter_summed, feat_summed), 'ctx')]
    pallas_call x1, Pallas kernels: 27.3 us -> 107 us  [fused(): pl.pallas_call(functools.partial(fused_kernel, reach, scale), out_shape=[...]
    ppermute x3 -> x0, waiting for transfers between devices: 38.5 us -> none  [from_behind(): return lax.ppermute(block, axis, route)]
    reduce_scatter x2 -> x0, waiting for transfers between devices: 23.5 us -> none  [the longest x1 13.2 us: per_device(): lax.psum_scatter(filter_part, 'dp', scatter_dimension=1, tiled=True)]
    ppermute x3 -> x0, starting transfers between devices: 9.15 us -> none  [from_behind(): return lax.ppermute(block, axis, route)]
    mul x2 -> x0, other arithmetic: 3.91 us -> none  [per_device(): return (filter_whole * scale, feat_whole * scale)]
    unnamed x10 -> x2, local copies, waits for them, and re-layouts: 1.34 us -> 3.91 us
  transfers between devices with their start and end apart: 7 -> 0, of which waited for: 4 -> 0; matrix products, arithmetic and copies ran while one was open for 1% -> 0% of each run, Pallas kernels for 0% -> 0%
where the time goes in v2:
time: 114 us; the launch traced here: 113 us
  Pallas kernels  107 us (94%)
  local copies, waits for them, and re-layouts  5.53 us (5%)
    pallas_call x1, Pallas kernels, fused(): pl.pallas_call(functools.partial(fused_kernel, reach, scale), out_shape=[...  107 us
    unnamed x2, local copies, waits for them, and re-layouts  3.91 us

profile of v2, /device:TPU:26, one launch (start us, length us, event | category | flops | bytes accessed | tf_op | source)
XLA Modules:
  0.0 112.8 jit_solution(16717213623989468336)
XLA Ops:
  0.6 1.6 %slice_bitcast_fusion.tail = bf16[8,12288]{1,0:T(8,128)(2,1)} fusion(bf16[1,128,12288]{2,1,0:T(8,128)(2,1)} %param.8), kind=kLoop, calls=%fused_computation | loop fusion | bytes 393216 | tf_op jit(solution)/shard_map/slice | solution.py:457
  2.2 106.6 %shard_map.95 = (f32[128,2048]{1,0:T(8,128)}, f32[7,6144]{1,0:T(8,128)}) custom-call(bf16[128,12288]{1,0:T(8,128)(2,1)} %bitcast.4, bf16[128,4096]{1,0:T(8,128)(2,1)} %bitcast.5, bf16[8,12288]{1,0:T(8,128)(2,1)} %slice_bitcast_fusion.tail, f32[128,2048]{1,0:T(8,128)} %taps_here.1, f32[7,6144]{1,0:T(8,128)} %w_here.1, bf16[256,256]{1,0:T(8,128)(2,1)} %constant.8.clone.m0, ...), custom_call_target="tpu_custom_call" | custom-call | tf_op jit(solution)/shard_map/pallas_call | solution.py:426
  108.8 2.3 %copy.12 = f32[128,2048]{1,0:T(8,128)} copy(f32[128,2048]{1,0:T(8,128)} %get-tuple-element.4) | data formatting | bytes 2097152
  111.1 1.6 %copy.13 = f32[7,6144]{1,0:T(8,128)} copy(f32[7,6144]{1,0:T(8,128)} %get-tuple-element.5) | data formatting | bytes 344064

commit v3 on v2

--- a/solution.py
+++ b/solution.py
@@ -186,13 +186,16 @@
 
 MESH = pl.DeviceIdType.MESH
 LANES = 128
+GROUP = 2
+PLANE = 4
 
 
 def fused_kernel(
-    reach, scale, x, up, tail, taps_here, w_here, m0, m1, m2, m3, filt_out, feat_out,
-    taps_all, w_all, prev, n_up, n_q, q_ext, k_ext, v_ext, up_ext,
+    reach, scale, x, up, taps_here, w_here, m0, m1, m2, m3, filt_out, feat_out,
+    taps_all, w_all, tail, prev, n_up, n_q, r_up, r_q, q_ext, k_ext, v_ext, up_ext,
     stage, dp_got, rs_send, rs_got, gathered,
     own_sem, swap_send, swap_got, tail_send, tail_got, halo_send, halo_got,
+    relay_send, relay_got,
     dp_send, dp_recv, rs_ssem, rs_rsem, ag_ssem, ag_rsem,
 ):
     n = lax.axis_size("ctx")
@@ -237,25 +240,65 @@
     def tail_copy():
         return remote(tail, prev, tail_send, tail_got, {"ctx": lax.rem(me + 1, n)})
 
-    def halo_copies(i, owner):
-        target = {"ctx": lax.rem(me + n - 1, n)}
+    groups = n // GROUP
+
+    def block_copies(g, first, sources, targets, send, got, device):
         copies = []
         for piece in range(2):
-            at = lanes_of(owner, piece)
-            for k, (src, dst) in enumerate(((up, n_up), (x, n_q))):
+            low = first * (GROUP * LANES) + piece * half
+            at = pl.ds(pl.multiple_of(low, LANES), GROUP * LANES)
+            for k, (src, dst) in enumerate(zip(sources, targets)):
                 s = 2 * piece + k
                 copies.append(
                     remote(
                         src.at[pl.ds(0, filt_rows), at], dst.at[:, at],
-                        halo_send.at[i, s], halo_got.at[i, s], target,
+                        send.at[g, s], got.at[g, s], {"ctx": device},
                     )
                 )
         return copies
 
+    head, landing, relay = (up, x), (n_up, n_q), (r_up, r_q)
+    near = (me > 0) & (lax.rem(me, PLANE) != 0)
+    far = (me > 0) & (lax.rem(me, PLANE) == 0)
+    relays = (lax.rem(me, PLANE) == 0) & (me < n - PLANE)
+
+    def near_copies(g):
+        back = lax.rem(me + n - 1, n)
+        return block_copies(
+            g, group_at(g, back), head, landing, halo_send, halo_got, back
+        )
+
+    def far_copies(g):
+        back = lax.rem(me + n - 1, n)
+        via = lax.rem(me + n - PLANE, n)
+        return block_copies(g, group_at(g, back), head, relay, halo_send, relay_got, via)
+
+    def arrivals(g):
+        return block_copies(
+            g, group_at(g, me), head, landing, halo_send, halo_got, lax.rem(me + 1, n)
+        )
+
+    def relay_arrivals(g):
+        end = lax.rem(me + PLANE - 1, n)
+        return block_copies(
+            g, group_at(g, end), head, relay, halo_send, relay_got, lax.rem(me + PLANE, n)
+        )
+
+    def relay_copies(g):
+        end = lax.rem(me + PLANE - 1, n)
+        return block_copies(
+            g, group_at(g, end), relay, landing, relay_send, halo_got, end
+        )
+
+    def group_at(g, device):
+        return lax.rem(g + 1 + device // GROUP, groups)
+
     sent, kept = swaps()
     for copy in kept:
         copy.start()
 
+    tail[...] = x[rows - PAD :, :]
+
     @pl.when(me == 0)
     def _():
         prev[...] = jnp.zeros_like(prev)
@@ -273,11 +316,18 @@
     def _():
         tail_copy().start()
 
-    @pl.when(me > 0)
-    def _():
-        @pl.loop(0, n)
-        def _(i):
-            for copy in halo_copies(i, lax.rem(i + me, n)):
+    @pl.when(near)
+    def _():
+        @pl.loop(0, groups)
+        def _(g):
+            for copy in near_copies(g):
+                copy.start()
+
+    @pl.when(far)
+    def _():
+        @pl.loop(0, groups)
+        def _(g):
+            for copy in far_copies(g):
                 copy.start()
 
     for copy in kept:
@@ -300,14 +350,21 @@
         )
 
     def owner_at(i):
-        return lax.rem(i + 1 + me, n)
+        return group_at(i // GROUP, me) * GROUP + lax.rem(i + 1 + me, GROUP)
 
     def compute(i):
         owner = owner_at(i)
 
-        @pl.when(me < n - 1)
+        @pl.when(relays & (lax.rem(i, GROUP) == 0))
         def _():
-            for copy in halo_copies(i, owner):
+            g = i // GROUP
+            for came, goes in zip(relay_arrivals(g), relay_copies(g)):
+                came.wait_recv()
+                goes.start()
+
+        @pl.when((me < n - 1) & (lax.rem(i, GROUP) == 0))
+        def _():
+            for copy in arrivals(i // GROUP):
                 copy.wait_recv()
 
         def both(ref, group):
@@ -392,11 +449,25 @@
     def _():
         tail_copy().wait_send()
 
-    @pl.when(me > 0)
-    def _():
-        @pl.loop(0, n)
-        def _(i):
-            for copy in halo_copies(i, lax.rem(i + me, n)):
+    @pl.when(near)
+    def _():
+        @pl.loop(0, groups)
+        def _(g):
+            for copy in near_copies(g):
+                copy.wait_send()
+
+    @pl.when(far)
+    def _():
+        @pl.loop(0, groups)
+        def _(g):
+            for copy in far_copies(g):
+                copy.wait_send()
+
+    @pl.when(relays)
+    def _():
+        @pl.loop(0, groups)
+        def _(g):
+            for copy in relay_copies(g):
                 copy.wait_send()
 
     @pl.loop(0, n)
@@ -429,12 +500,15 @@
             jax.ShapeDtypeStruct(filter_taps.shape, F32),
             jax.ShapeDtypeStruct(feat_weight.shape, F32),
         ],
-        in_specs=[pl.BlockSpec(memory_space=pltpu.VMEM)] * 9,
+        in_specs=[pl.BlockSpec(memory_space=pltpu.VMEM)] * 8,
         out_specs=[pl.BlockSpec(memory_space=pltpu.VMEM)] * 2,
         scratch_shapes=[
             pltpu.VMEM((filt_rows, channels), F32),
             pltpu.VMEM((reach, x.shape[1]), F32),
             pltpu.VMEM((PAD, x.shape[1]), BF16),
+            pltpu.VMEM((PAD, x.shape[1]), BF16),
+            pltpu.VMEM((filt_rows, channels), BF16),
+            pltpu.VMEM((filt_rows, channels), BF16),
             pltpu.VMEM((filt_rows, channels), BF16),
             pltpu.VMEM((filt_rows, channels), BF16),
             pltpu.VMEM((PAD + size, width), F32),
@@ -448,18 +522,20 @@
             pltpu.VMEM((n, packed, LANES), BF16),
             dma(2), dma(2), dma(2),
             pltpu.SemaphoreType.DMA, pltpu.SemaphoreType.DMA,
-            dma(n, 4), dma(n, 4),
+            *[dma(n // GROUP, 4)] * 4,
             dma(n), dma(n), dma(n), dma(n), dma(n), dma(n),
         ],
         compiler_params=pltpu.CompilerParams(
             collective_id=0, has_side_effects=True, vmem_limit_bytes=60 * 2**20
         ),
-    )(x, up, x[rows - PAD :], filter_taps, feat_weight, *mats)
+    )(x, up, filter_taps, feat_weight, *mats)
 
 
 def per_device(inputs, feat_weight, filter_taps, upstream):
-    cut = 2 * lax.axis_size("ctx") * LANES
-    if lax.axis_size("dp") == 2 and upstream.shape[2] == cut:
+    n = lax.axis_size("ctx")
+    cut = 2 * n * LANES
+    whole = n % GROUP == 0 and n % PLANE == 0 and PLANE % GROUP == 0
+    if lax.axis_size("dp") == 2 and upstream.shape[2] == cut and whole:
         return fused(inputs, feat_weight, filter_taps, upstream)
     return by_collectives(inputs, feat_weight, filter_taps, upstream)
 

time: 114 us -> 100 us (0.88); the launches traced: 113 us -> 100 us
  Pallas kernels: 107 us -> 95.7 us
  local copies, waits for them, and re-layouts: 5.53 us -> 3.91 us
    pallas_call x1, Pallas kernels: 107 us -> 95.7 us  [fused(): pl.pallas_call(functools.partial(fused_kernel, reach, scale), out_shape=[...]
    slice x1 -> x0, local copies, waits for them, and re-layouts: 1.62 us -> none  [fused(): x[rows - PAD:]]
where the time goes in v3:
time: 100 us
  Pallas kernels  95.7 us (96%)
  local copies, waits for them, and re-layouts  3.91 us (4%)
    pallas_call x1, Pallas kernels, fused(): pl.pallas_call(functools.partial(fused_kernel, reach, scale), out_shape=[...  95.7 us
    unnamed x2, local copies, waits for them, and re-layouts  3.91 us

profile of v3, /device:TPU:26, one launch (start us, length us, event | category | flops | bytes accessed | tf_op | source)
XLA Modules:
  0.0 100.2 jit_solution(13420681000548141748)
XLA Ops:
  0.6 95.7 %shard_map.95 = (f32[128,2048]{1,0:T(8,128)}, f32[7,6144]{1,0:T(8,128)}) custom-call(bf16[128,12288]{1,0:T(8,128)(2,1)} %bitcast.2, bf16[128,4096]{1,0:T(8,128)(2,1)} %bitcast.3, f32[128,2048]{1,0:T(8,128)} %taps_here.1, f32[7,6144]{1,0:T(8,128)} %w_here.1, bf16[256,256]{1,0:T(8,128)(2,1)} %constant.8.clone.m0, bf16[256,384]{1,0:T(8,128)(2,1)} %constant.9.clone.m1, ...), custom_call_target="tpu_custom_call" | custom-call | tf_op jit(solution)/shard_map/pallas_call | solution.py:497
  96.3 2.3 %copy.12 = f32[128,2048]{1,0:T(8,128)} copy(f32[128,2048]{1,0:T(8,128)} %get-tuple-element.4) | data formatting | bytes 2097152
  98.6 1.6 %copy.13 = f32[7,6144]{1,0:T(8,128)} copy(f32[7,6144]{1,0:T(8,128)} %get-tuple-element.5) | data formatting | bytes 344064

commit v4 on v3

--- a/solution.py
+++ b/solution.py
@@ -419,15 +419,35 @@
         total += rs_got[src].astype(F32)
     gathered[me] = total.astype(BF16)
 
-    def ag_copy(owner, target):
+    planes = n // PLANE
+
+    def ag_copy(k, q):
+        owner = lax.rem(me + k * PLANE, n)
+        target = me // PLANE * PLANE + lax.rem(me + q, PLANE)
         return remote(
-            gathered.at[owner], gathered.at[owner], ag_ssem.at[target], ag_rsem.at[owner],
+            gathered.at[owner], gathered.at[owner], ag_ssem.at[k, q], ag_rsem.at[owner],
             {"ctx": target},
         )
 
-    @pl.loop(1, n)
-    def _(j):
-        ag_copy(me, lax.rem(me + j, n)).start()
+    def ag_column(k):
+        return remote(
+            gathered.at[me], gathered.at[me], ag_ssem.at[k, 0], ag_rsem.at[me],
+            {"ctx": lax.rem(me + k * PLANE, n)},
+        )
+
+    def ag_arrival(owner):
+        return remote(
+            gathered.at[owner], gathered.at[owner], ag_ssem.at[0, 0], ag_rsem.at[owner],
+            {"ctx": lax.rem(me + 1, n)},
+        )
+
+    @pl.loop(1, planes)
+    def _(k):
+        ag_column(k).start()
+
+    @pl.loop(1, PLANE)
+    def _(q):
+        ag_copy(0, q).start()
 
     def unpack(owner):
         value = gathered[owner].astype(F32) * scale
@@ -439,11 +459,25 @@
 
     unpack(me)
 
-    @pl.loop(1, n)
-    def _(j):
-        src = lax.rem(me + j, n)
-        ag_copy(src, src).wait_recv()
+    @pl.loop(1, planes)
+    def _(k):
+        src = lax.rem(me + k * PLANE, n)
+        ag_arrival(src).wait_recv()
+
+        @pl.loop(1, PLANE)
+        def _(q):
+            ag_copy(k, q).start()
+
         unpack(src)
+
+    @pl.loop(0, planes)
+    def _(k):
+        @pl.loop(1, PLANE)
+        def _(q):
+            low = lax.rem(me // PLANE + k, planes) * PLANE
+            src = low + lax.rem(me + q, PLANE)
+            ag_arrival(src).wait_recv()
+            unpack(src)
 
     @pl.when(me < n - 1)
     def _():
@@ -478,9 +512,15 @@
     def _(i):
         rs_copy(i, owner_at(i)).wait_send()
 
-    @pl.loop(1, n)
-    def _(j):
-        ag_copy(me, lax.rem(me + j, n)).wait_send()
+    @pl.loop(1, planes)
+    def _(k):
+        ag_column(k).wait_send()
+
+    @pl.loop(0, planes)
+    def _(k):
+        @pl.loop(1, PLANE)
+        def _(q):
+            ag_copy(k, q).wait_send()
 
 
 def fused(inputs, feat_weight, filter_taps, upstream):
@@ -523,7 +563,7 @@
             dma(2), dma(2), dma(2),
             pltpu.SemaphoreType.DMA, pltpu.SemaphoreType.DMA,
             *[dma(n // GROUP, 4)] * 4,
-            dma(n), dma(n), dma(n), dma(n), dma(n), dma(n),
+            dma(n), dma(n), dma(n), dma(n), dma(n // PLANE, PLANE), dma(n),
         ],
         compiler_params=pltpu.CompilerParams(
             collective_id=0, has_side_effects=True, vmem_limit_bytes=60 * 2**20

time: 100 us -> 97.1 us (0.971); the launches traced: 100 us -> 95.7 us
  Pallas kernels: 95.7 us -> 91.2 us
    pallas_call x1, Pallas kernels: 95.7 us -> 91.2 us  [fused(): pl.pallas_call(functools.partial(fused_kernel, reach, scale), out_shape=[...]
where the time goes in v4:
time: 97.1 us; the launch traced here: 95.7 us
  Pallas kernels  91.2 us (94%)
  local copies, waits for them, and re-layouts  3.91 us (4%)
    pallas_call x1, Pallas kernels, fused(): pl.pallas_call(functools.partial(fused_kernel, reach, scale), out_shape=[...  91.2 us
    unnamed x2, local copies, waits for them, and re-layouts  3.91 us

profile of v4, /device:TPU:26, one launch (start us, length us, event | category | flops | bytes accessed | tf_op | source)
XLA Modules:
  0.0 95.7 jit_solution(4600832550120342596)
XLA Ops:
  0.6 91.2 %shard_map.95 = (f32[128,2048]{1,0:T(8,128)}, f32[7,6144]{1,0:T(8,128)}) custom-call(bf16[128,12288]{1,0:T(8,128)(2,1)} %bitcast.2, bf16[128,4096]{1,0:T(8,128)(2,1)} %bitcast.3, f32[128,2048]{1,0:T(8,128)} %taps_here.1, f32[7,6144]{1,0:T(8,128)} %w_here.1, bf16[256,256]{1,0:T(8,128)(2,1)} %constant.8.clone.m0, bf16[256,384]{1,0:T(8,128)(2,1)} %constant.9.clone.m1, ...), custom_call_target="tpu_custom_call" | custom-call | tf_op jit(solution)/shard_map/pallas_call | solution.py:537
  91.8 2.3 %copy.12 = f32[128,2048]{1,0:T(8,128)} copy(f32[128,2048]{1,0:T(8,128)} %get-tuple-element.4) | data formatting | bytes 2097152
  94.1 1.6 %copy.13 = f32[7,6144]{1,0:T(8,128)} copy(f32[7,6144]{1,0:T(8,128)} %get-tuple-element.5) | data formatting | bytes 344064

commit v5 on v4

--- a/solution.py
+++ b/solution.py
@@ -188,6 +188,7 @@
 LANES = 128
 GROUP = 2
 PLANE = 4
+AHEAD = 4
 
 
 def fused_kernel(
@@ -318,14 +319,14 @@
 
     @pl.when(near)
     def _():
-        @pl.loop(0, groups)
+        @pl.loop(0, min(AHEAD, groups))
         def _(g):
             for copy in near_copies(g):
                 copy.start()
 
     @pl.when(far)
     def _():
-        @pl.loop(0, groups)
+        @pl.loop(0, min(AHEAD, groups))
         def _(g):
             for copy in far_copies(g):
                 copy.start()
@@ -361,6 +362,16 @@
             for came, goes in zip(relay_arrivals(g), relay_copies(g)):
                 came.wait_recv()
                 goes.start()
+
+        @pl.when(near & (lax.rem(i, GROUP) == 0) & (i // GROUP + AHEAD < groups))
+        def _():
+            for copy in near_copies(i // GROUP + AHEAD):
+                copy.start()
+
+        @pl.when(far & (lax.rem(i, GROUP) == 0) & (i // GROUP + AHEAD < groups))
+        def _():
+            for copy in far_copies(i // GROUP + AHEAD):
+                copy.start()
 
         @pl.when((me < n - 1) & (lax.rem(i, GROUP) == 0))
         def _():

time: 97.1 us -> 97.3 us (level)
  no operation moved by 1% of the time
where the time goes in v5:
time: 97.3 us; the launch traced here: 95.9 us
  Pallas kernels  91.3 us (94%)
  local copies, waits for them, and re-layouts  3.91 us (4%)
    pallas_call x1, Pallas kernels, fused(): pl.pallas_call(functools.partial(fused_kernel, reach, scale), out_shape=[...  91.3 us
    unnamed x2, local copies, waits for them, and re-layouts  3.91 us

profile of v5, /device:TPU:26, one launch (start us, length us, event | category | flops | bytes accessed | tf_op | source)
XLA Modules:
  0.0 95.9 jit_solution(708574725736798290)
XLA Ops:
  0.6 91.3 %shard_map.95 = (f32[128,2048]{1,0:T(8,128)}, f32[7,6144]{1,0:T(8,128)}) custom-call(bf16[128,12288]{1,0:T(8,128)(2,1)} %bitcast.2, bf16[128,4096]{1,0:T(8,128)(2,1)} %bitcast.3, f32[128,2048]{1,0:T(8,128)} %taps_here.1, f32[7,6144]{1,0:T(8,128)} %w_here.1, bf16[256,256]{1,0:T(8,128)(2,1)} %constant.8.clone.m0, bf16[256,384]{1,0:T(8,128)(2,1)} %constant.9.clone.m1, ...), custom_call_target="tpu_custom_call" | custom-call | tf_op jit(solution)/shard_map/pallas_call | solution.py:548
  91.9 2.3 %copy.12 = f32[128,2048]{1,0:T(8,128)} copy(f32[128,2048]{1,0:T(8,128)} %get-tuple-element.4) | data formatting | bytes 2097152
  94.2 1.6 %copy.13 = f32[7,6144]{1,0:T(8,128)} copy(f32[7,6144]{1,0:T(8,128)} %get-tuple-element.5) | data formatting | bytes 344064
